TPU v7x, 32 devices: a whole 2x2x4 slice. The times are simulated.
32 devices in a mesh: seq: 16 (over z, x, core), tp: 2 (over y).
Axes of the slice: x: 2, y: 2, z: 4, core: 2. Of those that a mesh axis runs over, the one named last changes fastest.
Arguments:
- hidden: bfloat16 [8192, 4096], P('seq', 'tp'), may hold values from -6 to 6
- w_query: bfloat16 [4096, 4096], P(None, 'tp'), may hold values from -0.09375 to 0.09375
- w_key: bfloat16 [4096, 1024], P(None, 'tp'), may hold values from -0.09375 to 0.09375
- w_value: bfloat16 [4096, 1024], P(None, 'tp'), may hold values from -0.09375 to 0.09375
- w_out: bfloat16 [4096, 4096], P('tp'), may hold values from -0.09375 to 0.09375
- cache_keys: bfloat16 [256, 64, 1024], P('seq', None, 'tp'), may hold values from -52 to 52
- cache_values: bfloat16 [256, 64, 1024], P('seq', None, 'tp'), may hold values from -6 to 6
- cached_len: int32 [16], replicated, may hold values from 0 to 2048, as said below
- page_table: int32 [256, 2], P('seq'), may hold values from 0 to 31, as said below
Outputs:
- attn_out: bfloat16 [8192, 4096], P('seq', 'tp')
Inputs may be any that keep to these rules, and one draw needn't show every extreme that they name: `cached_len`: cached tokens of each request; some request has exactly 2048. `page_table`: row b is (r, j): pool block b holds request r's cached positions j * 64 to j * 64 + 63. Request r owns exactly ceil(cached_len[r] / 64) blocks, with places 0 to that count - 1, each once; every pool block is owned; the 16 blocks of one index of seq hold at most 2 blocks of any one request, and some index holds exactly 2 of some request.
All inputs are finite; a program needn't handle non-finite values.
Results may differ from a plain program's by a relative error of at most 0.019.
Values may be sent and summed in bfloat16 or wider, within the bound.
No kernel may reach another device: no remote copies, remote signals or barrier semaphores. Data moves between devices by JAX's collectives and lax.ppermute only.
A program may use at most 256 MiB of HBM per device.

v0:
```python
import math
import jax
import jax.numpy as jnp
from jax import lax
from jax.sharding import PartitionSpec as P

HD = 128
NEW = 512
CTX = 2048
ROPE_BASE = 1000000.0
masked_score = -1e30


def norm_rope(values, positions):
    values = values * lax.rsqrt(jnp.mean(values * values, axis=-1, keepdims=True) + 1e-06)
    half_width = values.shape[-1] // 2
    freqs = jnp.exp(
        jnp.arange(half_width, dtype=jnp.float32) * (-2.0 * math.log(ROPE_BASE) / values.shape[-1])
    )
    angles = positions.astype(jnp.float32)[:, None] * freqs[None, :]
    cosine = jnp.cos(angles)[:, None, :]
    sine = jnp.sin(angles)[:, None, :]
    first = values[..., :half_width]
    second = values[..., half_width:]
    return jnp.concatenate(
        [first * cosine - second * sine, second * cosine + first * sine], axis=-1
    )


def pick_rows(match, slot_count):
    ranking = jnp.cumsum(match.astype(jnp.int32)) - 1
    slot_ids = jnp.arange(slot_count, dtype=jnp.int32)
    chosen = match[None, :] & (ranking[None, :] == slot_ids[:, None])
    row_ids = jnp.arange(match.shape[0], dtype=jnp.int32)
    picked = jnp.sum(jnp.where(chosen, row_ids[None, :], 0), axis=1)
    present = jnp.any(chosen, axis=1)
    return (picked, present)


def on_device(
    hidden, w_query, w_key, w_value, w_out, cache_keys, cache_values, cached_len, page_table
):
    tokens_here = hidden.shape[0]
    query_heads = w_query.shape[1] // HD
    kv_heads = w_key.shape[1] // HD
    group = query_heads // kv_heads
    block_len = cache_keys.shape[1]
    width_kv = cache_keys.shape[2]
    span_count = NEW // tokens_here
    device = lax.axis_index("seq")
    request = device // span_count
    span = device % span_count
    length = cached_len[request]
    positions = length + span * tokens_here + jnp.arange(tokens_here, dtype=jnp.int32)
    piece = lax.all_gather(hidden, "tp", axis=1, tiled=True)

    def project(weight):
        return jnp.dot(piece, weight, preferred_element_type=jnp.float32)

    query_sum = project(w_query)
    key_sum = project(w_key)
    value_sum = project(w_value)
    queries = norm_rope(query_sum.reshape(tokens_here, query_heads, HD), positions).astype(
        jnp.bfloat16
    )
    grouped = (
        queries.reshape(tokens_here, kv_heads, group, HD)
        .transpose(1, 2, 0, 3)
        .reshape(kv_heads, group * tokens_here, HD)
    )
    fresh_keys = (
        norm_rope(key_sum.reshape(tokens_here, kv_heads, HD), positions)
        .astype(jnp.bfloat16)
        .reshape(tokens_here, kv_heads * HD)
    )
    fresh_values = value_sum.astype(jnp.bfloat16)
    row_query = span * tokens_here + jnp.arange(group * tokens_here, dtype=jnp.int32) % tokens_here

    def attend(state, keys, values, valid):
        keys = keys.reshape(-1, kv_heads, HD)
        values = values.reshape(-1, kv_heads, HD)
        scores = jnp.einsum(
            "krd,nkd->krn", grouped, keys, preferred_element_type=jnp.float32
        ) * HD ** (-0.5)
        scores = jnp.where(valid[None], scores, masked_score)
        running, total, accum = state
        newest = jnp.maximum(running, jnp.max(scores, axis=-1))
        weights = jnp.where(valid[None], jnp.exp(scores - newest[..., None]), 0.0)
        rescale = jnp.exp(running - newest)
        total = total * rescale + jnp.sum(weights, axis=-1)
        accum = accum * rescale[..., None] + jnp.einsum(
            "krn,nkd->krd", weights.astype(jnp.bfloat16), values, preferred_element_type=jnp.float32
        )
        return (newest, total, accum)

    state = (
        jnp.full((kv_heads, group * tokens_here), masked_score, jnp.float32),
        jnp.zeros((kv_heads, group * tokens_here), jnp.float32),
        jnp.zeros((kv_heads, group * tokens_here, HD), jnp.float32),
    )
    carry = state
    piece_keys = lax.all_gather(cache_keys[None], "seq", axis=0, tiled=True)
    piece_values = lax.all_gather(cache_values[None], "seq", axis=0, tiled=True)
    piece_table = lax.all_gather(page_table[None], "seq", axis=0, tiled=True)
    piece_fresh_k = lax.all_gather(fresh_keys[None], "seq", axis=0, tiled=True)
    piece_fresh_v = lax.all_gather(fresh_values[None], "seq", axis=0, tiled=True)
    source_count = piece_keys.shape[0]
    block_count = source_count * piece_keys.shape[1]
    per_peer = max(1, CTX // block_len // lax.axis_size("seq"))
    slot_count = min(block_count, source_count * per_peer)
    flat_table = piece_table.reshape(block_count, 2)
    places = flat_table[:, 1]
    match = (flat_table[:, 0] == request) & (places * block_len < length)
    picked, present = pick_rows(match, slot_count)
    keys_taken = piece_keys.reshape(block_count, block_len, width_kv)[picked].reshape(
        slot_count * block_len, width_kv
    )
    values_taken = piece_values.reshape(block_count, block_len, width_kv)[picked].reshape(
        slot_count * block_len, width_kv
    )
    key_pos = places[picked][:, None] * block_len + jnp.arange(block_len, dtype=jnp.int32)[None, :]
    valid = (present[:, None] & (key_pos < length)).reshape(1, slot_count * block_len)
    carry = attend(carry, keys_taken, values_taken, valid)
    sources = jnp.arange(source_count, dtype=jnp.int32)
    source_count = sources.shape[0]
    slot_count = min(source_count, span_count)
    match = (sources // span_count == request) & (sources % span_count <= span)
    picked, present = pick_rows(match, slot_count)
    keys_taken = piece_fresh_k[picked].reshape(slot_count * tokens_here, width_kv)
    values_taken = piece_fresh_v[picked].reshape(slot_count * tokens_here, width_kv)
    key_index = (sources[picked] % span_count)[:, None] * tokens_here + jnp.arange(
        tokens_here, dtype=jnp.int32
    )[None, :]
    live = jnp.broadcast_to(present[:, None], key_index.shape).reshape(-1)
    valid = live[None, :] & (key_index.reshape(-1)[None, :] <= row_query[:, None])
    state = attend(carry, keys_taken, values_taken, valid)
    running, total, accum = state
    attended = (accum / total[..., None]).astype(jnp.bfloat16)
    attended = (
        attended.reshape(kv_heads, group, tokens_here, HD)
        .transpose(2, 0, 1, 3)
        .reshape(tokens_here, query_heads * HD)
    )
    partial_out = jnp.dot(attended, w_out, preferred_element_type=jnp.float32)
    return lax.psum_scatter(partial_out.astype(jnp.bfloat16), "tp", scatter_dimension=1, tiled=True)


def solution(mesh):
    in_specs = (
        P("seq", "tp"),
        P(None, "tp"),
        P(None, "tp"),
        P(None, "tp"),
        P("tp", None),
        P("seq", None, "tp"),
        P("seq", None, "tp"),
        P(),
        P("seq", None),
    )
    out_specs = P("seq", "tp")
    return jax.shard_map(
        on_device, mesh=mesh, in_specs=in_specs, out_specs=out_specs, check_vma=False
    )
```

profile of v0, /device:TPU:0, one launch (start us, length us, event | category | flops | bytes accessed | tf_op | source)
XLA Modules:
  0.0 617.4 jit_solution(7555049823054470965)
XLA Ops:
  6.5 0.7 all-gather.11.cloned.1.call-update
  7.3 1.3 dynamic_slice.3
  8.6 0.6 add_convert_fusion.2
  9.2 0.5 multiply_cosine_fusion
  9.8 58.6 %all-gather.11.cloned.1.call-done = bf16[512,4096]{1,0:T(8,128)(2,1)} async-done(((bf16[512,2048]{1,0:T(8,128)(2,1)}), bf16[512,4096]{1,0:T(8,128)(2,1)}) %all-gather.11.cloned.1.call-update) | async-done | bytes 4194320 | tf_op jit(solution)/shard_map/all_gather | solution.py:55
  68.4 5.9 multiply_reduce_fusion.1
  74.3 0.1 broadcast_multiply_fusion.1
  74.4 0.2 subtract_convert_fusion.1
  74.6 1.0 copy.98
  75.7 0.0 all-gather.19.cloned.1.call-start
  75.7 6.6 %convolution_convert_fusion.1 = bf16[512,512]{1,0:T(8,128)(2,1)} fusion(bf16[512,4096]{1,0:T(8,128)(2,1)} %all-gather.11.cloned.1.call-done, bf16[4096,512]{1,0:T(8,128)(2,1)} %param.12), kind=kOutput, calls=%fused_computation.30 | convolution fusion | flops 2147745792 | bytes 8912896 | tf_op jit(solution)/shard_map/dot_general | solution.py:58
  82.3 0.0 all-gather.15.cloned.1.call-start
  82.4 0.5 all-gather.15.cloned.1.call-update
  83.0 0.5 all-gather.17.cloned.1.call-update
  83.5 0.1 copy.80
  83.7 0.1 copy.81
  83.8 21.8 %all-gather.4 = s32[16,16,2]{1,2,0:T(2,128)S(1)} all-gather(s32[1,16,2]{1,2,0:T(2,128)S(1)} %bitcast.60), channel_id=2, replica_groups=mesh['seq'=16,'tp'=2] {'seq'}, dimensions={0}, use_global_device_ids=true | all-gather | bytes 2176 | tf_op jit(solution)/shard_map/all_gather | solution.py:104
  105.6 0.1 reshape.412
  105.7 0.7 compare_reduce_fusion
  106.4 0.3 reduce-window.19
  106.7 0.1 slice.27
  106.8 0.1 slice_reduce_fusion
  106.9 0.6 compare_and_fusion.1
  107.6 0.1 add_bitcast_fusion
  107.6 0.1 select_reduce_fusion
  107.8 0.7 gather_fusion
  108.5 0.1 fusion.19
  108.6 0.7 fusion.20
  109.3 0.1 and.107
  109.5 0.1 fusion.24
  109.6 0.6 select_reduce_fusion.1
  112.0 0.6 fusion.33
  112.6 1.3 fusion.12
  113.9 12.9 %convolution_bitcast_fusion = f32[64,8,16,128]{3,1,2,0:T(8,128)S(1)} fusion(bf16[512,4096]{1,0:T(8,128)(2,1)} %all-gather.11.cloned.1.call-done, bf16[4096,2048]{1,0:T(8,128)(2,1)} %param.10), kind=kOutput, calls=%fused_computation.24 | convolution fusion | flops 8589934592 | bytes 25165824 | tf_op jit(solution)/shard_map/dot_general | solution.py:58
  126.9 0.9 copy.101
  127.8 2.0 copy-done
  129.8 1.2 multiply_reduce_fusion
  131.0 0.1 copy.78
  131.1 0.1 copy.79
  131.3 4.1 broadcast_multiply_fusion
  135.3 1.6 subtract_convert_fusion
  136.9 0.5 copy.82
  137.5 0.5 copy.83
  138.0 1.2 pad_maximum_fusion
  139.2 11.7 %all-gather.13.cloned.1.call-done = bf16[16,512,512]{2,1,0:T(8,128)(2,1)} async-done(((bf16[1,512,512]{2,1,0:T(8,128)(2,1)}), bf16[16,512,512]{2,1,0:T(8,128)(2,1)}) %all-gather.13.cloned.1.call-update) | async-done | bytes 8388624 | tf_op jit(solution)/shard_map/all_gather | solution.py:105
  150.8 75.4 %all-gather.19.cloned.1.call-done = bf16[8192,512]{1,0:T(8,128)(2,1)} async-done(((bf16[512,512]{1,0:T(8,128)(2,1)}), bf16[8192,512]{1,0:T(8,128)(2,1)}) %all-gather.19.cloned.1.call-update) | async-done | bytes 8388624 | tf_op jit(solution)/shard_map/all_gather | solution.py:106
  226.2 2.2 constant_dynamic-slice_fusion
  228.5 2.1 copy.99
  230.5 2.1 copy.100
  232.6 8.5 %fusion.6 = (f32[4,2048]{1,0:T(4,128)S(1)}, f32[4,2048,512]{1,2,0:T(8,128)}) fusion(pred[2048,512]{0,1:T(8,128)(4,1)S(1)} %fusion.12, bf16[4,2048,128]{2,1,0:T(8,128)(2,1)S(1)} %bitcast.49, bf16[512,4,128]{0,2,1:T(8,128)(2,1)} %bitcast.53), kind=kOutput, calls=%fused_computation.12 | convolution fusion | flops 1086316544 | bytes 20480000 | tf_op jit(solution)/shard_map/krd,nkd->krn/dot_general | solution.py:82
  241.1 112.3 %all-gather.15.cloned.1.call-done = bf16[256,64,512]{2,1,0:T(8,128)(2,1)} async-done(((bf16[16,64,512]{2,1,0:T(8,128)(2,1)}), bf16[256,64,512]{2,1,0:T(8,128)(2,1)}) %all-gather.15.cloned.1.call-update) | async-done | bytes 16777232 | tf_op jit(solution)/shard_map/all_gather | solution.py:102
  353.4 7.8 %gather_fusion.1 = bf16[32,64,512]{2,1,0:T(8,128)(2,1)} fusion(bf16[256,64,512]{2,1,0:T(8,128)(2,1)} %all-gather.15.cloned.1.call-done, s32[1024]{0:T(1024)S(1)} %pad_clamp_fusion), kind=kCustom, calls=%fused_computation.1 | custom fusion | bytes 4194432 | tf_op jit(solution)/shard_map/gather | solution.py:115
  361.2 4.1 reshape_reshape.12
  365.3 25.8 %fusion = (f32[4,2048]{1,0:T(4,128)S(1)}, f32[4,2048,2048]{1,2,0:T(8,128)}) fusion(pred[2048]{0:T(1024)(128)(4,1)S(1)} %and.107, bf16[4,2048,128]{2,1,0:T(8,128)(2,1)S(1)} %bitcast.50, bf16[2048,4,128]{2,1,0:T(4,128)(2,1)} %reshape_reshape.12), kind=kOutput, calls=%fused_computation.5 | convolution fusion | flops 4345290752 | bytes 71337984 | tf_op jit(solution)/shard_map/krd,nkd->krn/dot_general | solution.py:82
  391.1 8.1 %fusion.7 = f32[4,2048]{1,0:T(4,128)S(1)} fusion(f32[4,2048,512]{1,2,0:T(8,128)} %get-tuple-element.45, f32[4,2048]{1,0:T(4,128)S(1)} %get-tuple-element.34, pred[2048,512]{0,1:T(8,128)(4,1)S(1)} %fusion.12), kind=kLoop, calls=%fused_computation.13 | loop fusion | flops 20963328 | bytes 17891328 | tf_op jit(solution)/shard_map/reduce_sum | solution.py:90
  399.2 10.6 %fusion.9 = f32[4,2048,128]{2,1,0:T(8,128)} fusion(bf16[512,4,128]{0,2,1:T(8,128)(2,1)S(1)} %bitcast.57, f32[4,2048,512]{1,2,0:T(8,128)} %get-tuple-element.45, f32[4,2048]{1,0:T(4,128)S(1)} %get-tuple-element.34, pred[2048,512]{0,1:T(8,128)(4,1)S(1)} %fusion.12), kind=kOutput, calls=%fused_computation.15 | convolution fusion | flops 1094713344 | bytes 22577152 | tf_op jit(solution)/shard_map/krn,nkd->krd/dot_general | solution.py:91
  409.8 70.7 %all-gather.17.cloned.1.call-done = bf16[256,64,512]{2,1,0:T(8,128)(2,1)} async-done(((bf16[16,64,512]{2,1,0:T(8,128)(2,1)}), bf16[256,64,512]{2,1,0:T(8,128)(2,1)}) %all-gather.17.cloned.1.call-update) | async-done | bytes 16777232 | tf_op jit(solution)/shard_map/all_gather | solution.py:103
  480.5 6.4 %gather_fusion.2 = bf16[32,64,512]{2,1,0:T(8,128)(2,1)S(1)} fusion(bf16[256,64,512]{2,1,0:T(8,128)(2,1)} %all-gather.17.cloned.1.call-done, s32[1024]{0:T(1024)S(1)} %pad_clamp_fusion), kind=kCustom, calls=%fused_computation.2 | custom fusion | bytes 4194432 | tf_op jit(solution)/shard_map/gather | solution.py:118
  487.0 2.0 reshape_reshape.13
  489.0 21.6 %fusion.1 = f32[4,2048]{1,0:T(4,128)S(1)} fusion(f32[4,2048,2048]{1,2,0:T(8,128)} %get-tuple-element.43, f32[4,2048]{1,0:T(4,128)S(1)} %get-tuple-element.35, pred[2048]{0:T(1024)(128)(4,1)S(1)} %and.107), kind=kLoop, calls=%fused_computation.6 | loop fusion | flops 83877888 | bytes 67176448 | tf_op jit(solution)/shard_map/reduce_sum | solution.py:90
  510.7 30.3 %divide_convert_fusion = bf16[4,2048,128]{2,1,0:T(8,128)(2,1)} fusion(f32[4,2048,128]{2,1,0:T(8,128)} %fusion.9, f32[4,2048,2048]{1,2,0:T(8,128)} %get-tuple-element.43, f32[4,2048]{1,0:T(4,128)S(1)} %get-tuple-element.35, pred[2048]{0:T(1024)(128)(4,1)S(1)} %and.107, bf16[2048,4,128]{2,1,0:T(4,128)(2,1)S(1)} %copy-done.1, ...), kind=kOutput, calls=%fused_computation.18 | convolution fusion | flops 4384096256 | bytes 75630592 | tf_op jit(solution)/shard_map/krn,nkd->krd/dot_general | solution.py:91
  541.0 2.8 copy.93
  543.8 13.9 %convolution_convert_fusion = bf16[512,4096]{1,0:T(8,128)(2,1)} fusion(bf16[512,2048]{0,1:T(8,128)(2,1)S(1)} %bitcast.55, bf16[2048,4096]{1,0:T(8,128)(2,1)} %param.13), kind=kOutput, calls=%fused_computation.17 | convolution fusion | flops 8592031744 | bytes 23068672 | tf_op jit(solution)/shard_map/dot_general | solution.py:144
  557.7 52.6 %reduce-scatter.2.cloned.1.call-done = bf16[512,2048]{1,0:T(8,128)(2,1)} async-done(((bf16[512,4096]{1,0:T(8,128)(2,1)}), bf16[512,2048]{1,0:T(8,128)(2,1)}) %reduce-scatter.2.cloned.1.call-update) | async-done | bytes 2097168 | tf_op jit(solution)/shard_map/reduce_scatter | solution.py:145
  (29 shorter events, 0.4 us)
Async XLA Ops:
  6.5 61.8 %all-gather.11.cloned.1.call-start = ((), (), s32[]{:S(2)}) async-start(), calls=%async_computation.1 | async-start | bytes 6291456 | tf_op jit(solution)/shard_map/all_gather | solution.py:55
  7.3 143.6 %all-gather.13.cloned.1.call-start = ((), (), s32[]{:S(2)}) async-start(), calls=%async_computation.2 | async-start | bytes 8912896 | tf_op jit(solution)/shard_map/all_gather | solution.py:105
  75.7 8.2 %copy-start.3 = (s32[16,2]{0,1:T(2,128)S(1)}, s32[16,2]{0,1:T(2,128)}, u32[]{:S(2)}) copy-start(s32[16,2]{0,1:T(2,128)} %param.17) | copy-start | bytes 388
  75.7 150.5 %all-gather.19.cloned.1.call-start = ((), (), s32[]{:S(2)}) async-start(), calls=%async_computation.6 | async-start | bytes 8912896 | tf_op jit(solution)/shard_map/all_gather | solution.py:106
  82.3 271.1 %all-gather.15.cloned.1.call-start = ((), (), s32[]{:S(2)}) async-start(), calls=%async_computation.4 | async-start | bytes 17825792 | tf_op jit(solution)/shard_map/all_gather | solution.py:102
  82.9 397.6 %all-gather.17.cloned.1.call-start = ((), (), s32[]{:S(2)}) async-start(), calls=%async_computation.5 | async-start | bytes 17825792 | tf_op jit(solution)/shard_map/all_gather | solution.py:103
  83.5 526.8 %reduce-scatter.2.cloned.1.call-start = ((), (), s32[]{:S(2)}) async-start(), calls=%async_computation.3 | async-start | bytes 6291456 | tf_op jit(solution)/shard_map/reduce_scatter | solution.py:145
  127.8 2.0 copy-start
  391.1 8.1 %copy-start.2 = (bf16[1,512,512]{1,2,0:T(8,128)(2,1)S(1)}, bf16[1,512,512]{1,2,0:T(8,128)(2,1)}, u32[]{:S(2)}) copy-start(bf16[1,512,512]{1,2,0:T(8,128)(2,1)} %copy.100) | copy-start | bytes 1572868
  489.0 21.7 %copy-start.1 = (bf16[2048,4,128]{2,1,0:T(4,128)(2,1)S(1)}, bf16[2048,4,128]{2,1,0:T(4,128)(2,1)}, u32[]{:S(2)}) copy-start(bf16[2048,4,128]{2,1,0:T(4,128)(2,1)} %reshape_reshape.13) | copy-start | bytes 6291460
Sparse Core Ops, SparseCore 0:
  8.9 59.4 all-gather.10
  75.8 75.0 all-gather.12
  153.0 73.1 all-gather.18
  228.2 125.1 all-gather.14
  355.4 125.0 all-gather.16
  557.8 52.4 reduce-scatter.1
where the time goes:
time: 622 us; the launch traced here: 617 us
  waiting for transfers between devices  383 us (62%)
  matrix products  114 us (18%)
  other arithmetic  44.7 us (7%)
  local copies, waits for them, and re-layouts  37.4 us (6%)
  blocking collectives  21.8 us (4%)
  between operations  15.7 us (3%)
    all_gather x1, waiting for transfers between devices, on_device(): piece_keys = lax.all_gather(cache_keys[None], 'seq', axis=0, tiled=True)  112 us
    all_gather x1, waiting for transfers between devices, on_device(): lax.all_gather(fresh_values[None], 'seq', axis=0, tiled=True)  75.4 us
    all_gather x1, waiting for transfers between devices, on_device(): piece_values = lax.all_gather(cache_values[None], 'seq', axis=0, tiled=True)  70.7 us
    all_gather x1, waiting for transfers between devices, on_device(): piece = lax.all_gather(hidden, 'tp', axis=1, tiled=True)  58.6 us
    reduce_scatter x1, waiting for transfers between devices, on_device(): lax.psum_scatter(partial_out.astype(jnp.bfloat16), 'tp', scatter_dimensio...  52.6 us
    dot_general x2, matrix products, attend(): jnp.einsum('krn,nkd->krd', weights.astype(jnp.bfloat16), values, preferre...  40.8 us
    dot_general x2, matrix products, attend(): jnp.einsum('krd,nkd->krn', grouped, keys, preferred_element_type=jnp.floa...  34.3 us
    reduce_sum x2, other arithmetic, attend(): total = total * rescale + jnp.sum(weights, axis=-1)  29.7 us
  transfers between devices with their start and end apart: 6, of which 6 were waited for; matrix products, arithmetic and copies ran while one was open for 18% of the time, Pallas kernels for 0%

commit v1 on v0

--- a/solution.py
+++ b/solution.py
@@ -9,6 +9,18 @@
 CTX = 2048
 ROPE_BASE = 1000000.0
 masked_score = -1e30
+
+
+def doubled_up(x, axis, dim):
+    ways, here, step = (lax.axis_size(axis), lax.axis_index(axis), x.shape[dim])
+    line, have = (x, 1)
+    while have < ways:
+        line = jnp.concatenate(
+            [line, lax.ppermute(line, axis, [(d, (d - have) % ways) for d in range(ways)])],
+            axis=dim,
+        )
+        have = 2 * have
+    return jnp.roll(line, here * step, axis=dim)
 
 
 def norm_rope(values, positions):
@@ -99,7 +111,7 @@
         jnp.zeros((kv_heads, group * tokens_here, HD), jnp.float32),
     )
     carry = state
-    piece_keys = lax.all_gather(cache_keys[None], "seq", axis=0, tiled=True)
+    piece_keys = doubled_up(cache_keys[None], "seq", 0)
     piece_values = lax.all_gather(cache_values[None], "seq", axis=0, tiled=True)
     piece_table = lax.all_gather(page_table[None], "seq", axis=0, tiled=True)
     piece_fresh_k = lax.all_gather(fresh_keys[None], "seq", axis=0, tiled=True)

time: 622 us -> 1060 us (1.70)
  waiting for transfers between devices: 383 us -> 652 us
  blocking collectives: 21.8 us -> 121 us
  local copies, waits for them, and re-layouts: 37.4 us -> 89.3 us
    ppermute x0 -> x4, waiting for transfers between devices: none -> 539 us  [doubled_up(): lax.ppermute(line, axis, [(d, (d - have) % ways) for d in range(ways)])]
    all_gather x1 -> x0, waiting for transfers between devices: 112 us -> none  [on_device(): piece_keys = lax.all_gather(cache_keys[None], 'seq', axis=0, tiled=True)]
    all_gather x1, blocking collectives: 21.8 us -> 121 us  [on_device(): piece_table = lax.all_gather(page_table[None], 'seq', axis=0, tiled=True)]
    all_gather x1, waiting for transfers between devices: 75.4 us -> 0.02 us  [on_device(): lax.all_gather(fresh_values[None], 'seq', axis=0, tiled=True)]
    all_gather x1, waiting for transfers between devices: 70.7 us -> 0.01 us  [on_device(): piece_values = lax.all_gather(cache_values[None], 'seq', axis=0, tiled=True)]
    unnamed x12 -> x35, local copies, waits for them, and re-layouts: 7.19 us -> 35.3 us
    dynamic_slice x0 -> x1, local copies, waits for them, and re-layouts: none -> 14 us  [doubled_up(): return jnp.roll(line, here * step, axis=dim)]
    all_gather x1, waiting for transfers between devices: 11.7 us -> 0.02 us  [on_device(): piece_fresh_k = lax.all_gather(fresh_keys[None], 'seq', axis=0, tiled=True)]
  transfers between devices with their start and end apart: 6 -> 9, of which waited for: 6 -> 5; matrix products, arithmetic and copies ran while one was open for 18% -> 18% of each run, Pallas kernels for 0% -> 0%
where the time goes in v1:
time: 1060 us; the launch traced here: 1050 us
  waiting for transfers between devices  652 us (62%)
  blocking collectives  121 us (11%)
  matrix products  109 us (10%)
  local copies, waits for them, and re-layouts  89.3 us (8%)
  other arithmetic  54.2 us (5%)
  between operations  15.6 us (1%)
    ppermute x4, waiting for transfers between devices, doubled_up(): lax.ppermute(line, axis, [(d, (d - have) % ways) for d in range(ways)])  539 us
    all_gather x1, blocking collectives, on_device(): piece_table = lax.all_gather(page_table[None], 'seq', axis=0, tiled=True)  121 us
    all_gather x1, waiting for transfers between devices, on_device(): piece = lax.all_gather(hidden, 'tp', axis=1, tiled=True)  58.6 us
    reduce_scatter x1, waiting for transfers between devices, on_device(): lax.psum_scatter(partial_out.astype(jnp.bfloat16), 'tp', scatter_dimensio...  53.4 us
    dot_general x2, matrix products, attend(): jnp.einsum('krn,nkd->krd', weights.astype(jnp.bfloat16), values, preferre...  40.5 us
    unnamed x35, local copies, waits for them, and re-layouts  35.3 us
    dot_general x2, matrix products, attend(): jnp.einsum('krd,nkd->krn', grouped, keys, preferred_element_type=jnp.floa...  29.6 us
    reduce_sum x2, other arithmetic, attend(): total = total * rescale + jnp.sum(weights, axis=-1)  25.8 us
  transfers between devices with their start and end apart: 9, of which 5 were waited for; matrix products, arithmetic and copies ran while one was open for 18% of the time, Pallas kernels for 0%

profile of v1, /device:TPU:0, one launch (start us, length us, event | category | flops | bytes accessed | tf_op | source)
XLA Modules:
  0.0 1049.5 jit_solution(10125449172548144068)
XLA Ops:
  6.5 0.7 all-gather.9.cloned.1.call-update
  7.3 1.2 dynamic_slice.7
  8.6 0.7 add_convert_fusion.2
  9.2 0.5 multiply_cosine_fusion
  9.8 58.6 %all-gather.9.cloned.1.call-done = bf16[512,4096]{1,0:T(8,128)(2,1)} async-done(((bf16[512,2048]{1,0:T(8,128)(2,1)}), bf16[512,4096]{1,0:T(8,128)(2,1)}) %all-gather.9.cloned.1.call-update) | async-done | bytes 4194320 | tf_op jit(solution)/shard_map/all_gather | solution.py:67
  68.4 5.9 multiply_reduce_fusion.1
  74.6 1.0 copy.97
  75.7 6.7 convolution_convert_fusion.1
  82.4 3.7 collective-permute-start
  86.2 26.5 %collective-permute-done = bf16[1,16,64,512]{3,2,1,0:T(8,128)(2,1)S(1)} collective-permute-done((bf16[1,16,64,512]{3,2,1,0:T(8,128)(2,1)S(1)}, bf16[1,16,64,512]{3,2,1,0:T(8,128)(2,1)S(1)}, u32[]{:S(2)}, u32[]{:S(2)}) %collective-permute-start) | collective-permute-done | bytes 1048608 | tf_op jit(solution)/shard_map/ppermute | solution.py:19
  112.8 1.0 copy-done.3
  114.0 76.0 %collective-permute-done.1 = bf16[2,16,64,512]{3,2,1,0:T(8,128)(2,1)S(1)} collective-permute-done((bf16[2,16,64,512]{3,2,1,0:T(8,128)(2,1)S(1)}, bf16[2,16,64,512]{3,2,1,0:T(8,128)(2,1)S(1)}, u32[]{:S(2)}, u32[]{:S(2)}) %collective-permute-start.1) | collective-permute-done | bytes 2097184 | tf_op jit(solution)/shard_map/ppermute | solution.py:19
  190.0 3.2 pad_maximum_fusion.1
  193.2 4.5 collective-permute-start.2
  197.7 0.8 copy.79
  198.7 121.1 %all-gather.3 = s32[16,16,2]{1,2,0:T(2,128)S(1)} all-gather(s32[1,16,2]{1,2,0:T(2,128)S(1)} %bitcast.69), channel_id=2, replica_groups=mesh['seq'=16,'tp'=2] {'seq'}, dimensions={0}, use_global_device_ids=true | all-gather | bytes 2176 | tf_op jit(solution)/shard_map/all_gather | solution.py:116
  319.9 0.7 compare_reduce_fusion
  320.6 0.7 compare_and_fusion.1
  321.2 6.8 pad_maximum_fusion
  328.7 0.7 gather_fusion
  329.6 0.7 fusion.20
  330.6 0.6 select_reduce_fusion.1
  333.1 0.6 fusion.33
  333.8 1.1 constant_dynamic-update-slice_fusion.9
  334.9 2.5 fusion.12
  337.4 2.4 constant_dynamic-update-slice_fusion.8
  339.8 1.5 constant_dynamic-update-slice_fusion.7
  341.2 11.7 %convolution_bitcast_fusion = f32[64,8,16,128]{3,1,2,0:T(8,128)S(1)} fusion(bf16[512,4096]{1,0:T(8,128)(2,1)S(1)} %copy-done.10, bf16[4096,2048]{1,0:T(8,128)(2,1)} %param.10), kind=kOutput, calls=%fused_computation.26 | convolution fusion | flops 8589934592 | bytes 25165824 | tf_op jit(solution)/shard_map/dot_general | solution.py:70
  352.9 0.9 copy.100
  353.9 1.9 copy-done.1
  355.8 1.9 multiply_reduce_fusion
  357.7 1.0 copy.77
  358.7 0.8 copy.78
  359.6 4.1 broadcast_multiply_fusion
  363.7 1.6 subtract_convert_fusion
  365.3 0.5 copy.81
  365.8 0.5 copy.82
  366.4 2.5 pad_maximum_fusion.2
  368.8 4.8 constant_dynamic-update-slice_fusion.6
  373.6 436.5 %collective-permute-done.3 = bf16[8,16,64,512]{3,2,1,0:T(8,128)(2,1)} collective-permute-done((bf16[8,16,64,512]{3,2,1,0:T(8,128)(2,1)}, bf16[8,16,64,512]{3,2,1,0:T(8,128)(2,1)}, u32[]{:S(2)}, u32[]{:S(2)}) %collective-permute-start.3) | collective-permute-done | bytes 8388640 | tf_op jit(solution)/shard_map/ppermute | solution.py:19
  810.1 7.7 constant_dynamic-update-slice_fusion.5
  817.8 1.1 constant_dynamic-update-slice_fusion.4
  818.9 1.1 constant_dynamic-update-slice_fusion.3
  820.1 1.5 constant_dynamic-update-slice_fusion.2
  821.5 4.7 constant_dynamic-update-slice_fusion.1
  826.2 7.7 constant_dynamic-update-slice_fusion
  833.9 14.0 %constant_dynamic-slice_fusion.2 = bf16[16,16,64,512]{3,2,1,0:T(8,128)(2,1)} fusion(bf16[32,16,64,512]{3,2,1,0:T(8,128)(2,1)} %constant_dynamic-update-slice_fusion, s32[]{:T(128)S(6)} %select_n.104), kind=kLoop, calls=%fused_computation.83 | loop fusion | bytes 33554436 | tf_op jit(solution)/shard_map/jit(_roll_dynamic)/dynamic_slice | solution.py:23
  847.9 7.9 gather_fusion.1
  855.8 4.1 reshape_reshape.12
  859.9 25.0 %fusion = (f32[4,2048]{1,0:T(4,128)S(1)}, f32[4,2048,2048]{1,2,0:T(8,128)}) fusion(pred[2048]{0:T(1024)(128)(4,1)S(1)} %and.113, bf16[4,2048,128]{2,1,0:T(8,128)(2,1)S(1)} %bitcast.58, bf16[2048,4,128]{2,1,0:T(4,128)(2,1)} %reshape_reshape.12), kind=kOutput, calls=%fused_computation.5 | convolution fusion | flops 4345290752 | bytes 71337984 | tf_op jit(solution)/shard_map/krd,nkd->krn/dot_general | solution.py:94
  885.0 2.3 constant_dynamic-slice_fusion
  887.3 2.1 copy.98
  889.3 2.1 copy.99
  891.4 4.6 fusion.6
  896.1 4.2 fusion.7
  900.3 1.5 copy-done
  901.8 21.6 %fusion.1 = f32[4,2048]{1,0:T(4,128)S(1)} fusion(f32[4,2048,2048]{1,2,0:T(8,128)} %get-tuple-element.43, f32[4,2048]{1,0:T(4,128)S(1)} %get-tuple-element.35, pred[2048]{0:T(1024)(128)(4,1)S(1)} %and.113), kind=kLoop, calls=%fused_computation.6 | loop fusion | flops 83877888 | bytes 67176448 | tf_op jit(solution)/shard_map/reduce_sum | solution.py:102
  923.4 10.5 %fusion.9 = f32[4,2048,128]{2,1,0:T(8,128)} fusion(bf16[512,4,128]{0,2,1:T(8,128)(2,1)S(1)} %bitcast.66, f32[4,2048,512]{1,2,0:T(8,128)} %copy-done, f32[4,2048]{1,0:T(4,128)S(1)} %get-tuple-element.34, pred[2048,512]{0,1:T(8,128)(4,1)S(1)} %copy-done.6), kind=kOutput, calls=%fused_computation.16 | convolution fusion | flops 1094713344 | bytes 22577152 | tf_op jit(solution)/shard_map/krn,nkd->krd/dot_general | solution.py:103
  934.0 6.4 gather_fusion.2
  940.4 2.0 reshape_reshape.13
  942.5 29.9 %divide_convert_fusion = bf16[4,2048,128]{2,1,0:T(8,128)(2,1)S(1)} fusion(f32[4,2048,128]{2,1,0:T(8,128)} %fusion.9, f32[4,2048,2048]{1,2,0:T(8,128)} %get-tuple-element.43, f32[4,2048]{1,0:T(4,128)S(1)} %get-tuple-element.35, pred[2048]{0:T(1024)(128)(4,1)S(1)} %and.113, bf16[2048,4,128]{2,1,0:T(4,128)(2,1)} %reshape_reshape.13, ...), kind=kOutput, calls=%fused_computation.20 | convolution fusion | flops 4384096256 | bytes 75630592 | tf_op jit(solution)/shard_map/krn,nkd->krd/dot_general | solution.py:103
  972.4 2.3 copy.92
  974.7 14.5 %convolution_convert_fusion = bf16[512,4096]{1,0:T(8,128)(2,1)} fusion(bf16[512,2048]{0,1:T(8,128)(2,1)} %bitcast.64, bf16[2048,4096]{1,0:T(8,128)(2,1)} %param.13), kind=kOutput, calls=%fused_computation.18 | convolution fusion | flops 8592031744 | bytes 23068672 | tf_op jit(solution)/shard_map/dot_general | solution.py:156
  989.3 53.4 %reduce-scatter.2.cloned.1.call-done = bf16[512,2048]{1,0:T(8,128)(2,1)} async-done(((bf16[512,4096]{1,0:T(8,128)(2,1)}), bf16[512,2048]{1,0:T(8,128)(2,1)}) %reduce-scatter.2.cloned.1.call-update) | async-done | bytes 2097168 | tf_op jit(solution)/shard_map/reduce_scatter | solution.py:157
  (62 shorter events, 2.4 us)
Async XLA Ops:
  6.5 61.8 %all-gather.9.cloned.1.call-start = ((), (), s32[]{:S(2)}) async-start(), calls=%async_computation.1 | async-start | bytes 6291456 | tf_op jit(solution)/shard_map/all_gather | solution.py:67
  7.3 877.7 %all-gather.11.cloned.1.call-start = ((), (), s32[]{:S(2)}) async-start(), calls=%async_computation.2 | async-start | bytes 8912896 | tf_op jit(solution)/shard_map/all_gather | solution.py:117
  75.6 6.8 copy-start.2
  75.6 809.3 %all-gather.15.cloned.1.call-start = ((), (), s32[]{:S(2)}) async-start(), calls=%async_computation.5 | async-start | bytes 8912896 | tf_op jit(solution)/shard_map/all_gather | solution.py:118
  82.4 851.6 %all-gather.13.cloned.1.call-start = ((), (), s32[]{:S(2)}) async-start(), calls=%async_computation.4 | async-start | bytes 17825792 | tf_op jit(solution)/shard_map/all_gather | solution.py:115
  82.4 30.3 %collective-permute-start = (bf16[1,16,64,512]{3,2,1,0:T(8,128)(2,1)S(1)}, bf16[1,16,64,512]{3,2,1,0:T(8,128)(2,1)S(1)}, u32[]{:S(2)}, u32[]{:S(2)}) collective-permute-start(bf16[1,16,64,512]{3,2,1,0:T(8,128)(2,1)S(1)} %bitcast.53), channel_id=1, source_target_pairs={{0,30},{2,0},{4,2},{6,4},{8,6},{10,8},{12,10},{14,12},{16,14},{18,... | collective-permute-start | bytes 3145736 | tf_op jit(solution)/shard_map/ppermute | solution.py:19
  86.2 956.5 %reduce-scatter.2.cloned.1.call-start = ((), (), s32[]{:S(2)}) async-start(), calls=%async_computation.3 | async-start | bytes 6291456 | tf_op jit(solution)/shard_map/reduce_scatter | solution.py:157
  112.8 1.0 copy-start.3
  113.9 84.8 %copy-start.9 = (s32[16,2]{0,1:T(2,128)S(1)}, s32[16,2]{0,1:T(2,128)}, u32[]{:S(2)}) copy-start(s32[16,2]{0,1:T(2,128)} %param.17) | copy-start | bytes 388
  113.9 76.1 %collective-permute-start.1 = (bf16[2,16,64,512]{3,2,1,0:T(8,128)(2,1)S(1)}, bf16[2,16,64,512]{3,2,1,0:T(8,128)(2,1)S(1)}, u32[]{:S(2)}, u32[]{:S(2)}) collective-permute-start(bf16[2,16,64,512]{3,2,1,0:T(8,128)(2,1)S(1)} %pad_maximum_fusion.3), channel_id=1, source_target_pairs={{0,28},{2,30},{4,0},{6,2},{8,4},{10,6},{12,8},{14,10},{16,12},{18,... | collective-permute-start | bytes 6291464 | tf_op jit(solution)/shard_map/ppermute | solution.py:19
  193.2 128.0 %collective-permute-start.2 = (bf16[4,16,64,512]{3,2,1,0:T(8,128)(2,1)}, bf16[4,16,64,512]{3,2,1,0:T(8,128)(2,1)}, u32[]{:S(2)}, u32[]{:S(2)}) collective-permute-start(bf16[4,16,64,512]{3,2,1,0:T(8,128)(2,1)} %pad_maximum_fusion.1), channel_id=1, source_target_pairs={{0,24},{2,26},{4,28},{6,30},{8,0},{10,2},{12,4},{14,6},{16,8},{18,... | collective-permute-start | bytes 12582920 | tf_op jit(solution)/shard_map/ppermute | solution.py:19
  328.0 482.1 %collective-permute-start.3 = (bf16[8,16,64,512]{3,2,1,0:T(8,128)(2,1)}, bf16[8,16,64,512]{3,2,1,0:T(8,128)(2,1)}, u32[]{:S(2)}, u32[]{:S(2)}) collective-permute-start(bf16[8,16,64,512]{3,2,1,0:T(8,128)(2,1)} %pad_maximum_fusion), channel_id=1, source_target_pairs={{0,16},{2,18},{4,20},{6,22},{8,24},{10,26},{12,28},{14,30},{16,0},... | collective-permute-start | bytes 25165832 | tf_op jit(solution)/shard_map/ppermute | solution.py:19
  334.9 6.4 copy-start.10
  353.9 2.0 copy-start.1
  359.6 4.1 copy-start.7
  373.6 445.3 %copy-start.4 = (bf16[1,16,64,512]{3,2,1,0:T(8,128)(2,1)S(1)}, bf16[1,16,64,512]{3,2,1,0:T(8,128)(2,1)}, u32[]{:S(2)}) copy-start(bf16[1,16,64,512]{3,2,1,0:T(8,128)(2,1)} %copy-done.3) | copy-start | bytes 3145732
  847.9 12.0 %copy-start.5 = (bf16[512,4,4,128]{3,0,2,1:T(8,128)(2,1)S(1)}, bf16[512,4,4,128]{3,0,2,1:T(8,128)(2,1)}, u32[]{:S(2)}) copy-start(bf16[512,4,4,128]{3,0,2,1:T(8,128)(2,1)} %pad_maximum_fusion.2) | copy-start | bytes 6291460
  884.9 6.5 copy-start.6
  896.0 5.8 copy-start
  901.8 21.6 %copy-start.8 = (bf16[1,512,512]{1,2,0:T(8,128)(2,1)S(1)}, bf16[1,512,512]{1,2,0:T(8,128)(2,1)}, u32[]{:S(2)}) copy-start(bf16[1,512,512]{1,2,0:T(8,128)(2,1)} %copy.99) | copy-start | bytes 1572868
Sparse Core Ops, SparseCore 0:
  8.9 59.4 all-gather.8
  75.8 113.8 all-gather.10
  191.8 347.2 all-gather.14
  541.2 175.5 all-gather.12
  989.4 53.2 reduce-scatter.1
